TPU v7x, 32 devices: a whole 2x2x4 slice. The times are simulated.
32 devices in a mesh: row: 4 (over z), col: 8 (over y, x, core).
Axes of the slice: x: 2, y: 2, z: 4, core: 2. Of those that a mesh axis runs over, the one named last changes fastest.
Arguments:
- rhs_panels: float32 [3, 4, 8, 64, 256], P(None, 'row', 'col'), may hold values from -6 to 6
- inverse_diag: bfloat16 [3, 4, 8, 256, 256], P(None, 'row', 'col'), may hold values from -0.375 to 0.375
- factor_blocks: bfloat16 [3, 4, 80, 256, 256], P(None, 'row', 'col'), may hold values from -0.078125 to 0.078125
- block_target: int32 [3, 4, 80], P(None, 'row', 'col'), may hold values from 0 to 3, as said below
- block_source: int32 [3, 4, 80], P(None, 'row', 'col'), may hold values from 0 to 7, as said below
Outputs:
- solution: float32 [3, 4, 8, 64, 256], P(None, 'row', 'col')
Inputs may be any that keep to these rules, and one draw needn't show every extreme that they name: (block_target[p, r, q] - r) modulo 4 is below 2, or equals 2, or equals 3; each of 1, 2 and 3 occurs. (block_source[p, r, q] - q // 10) modulo 8 is below 2, or equals 4, or equals 7; each of 1, 4 and 7 occurs.
All inputs are finite; a program needn't handle non-finite values.
Results may differ from a plain program's by a relative error of at most 0.014.
Values may be sent and summed in bfloat16 or wider, within the bound.
A program may use at most 64 MiB of HBM per device.

v0:
```python
import jax
import jax.numpy as jnp
from jax import lax
from jax.sharding import PartitionSpec as P

WINDOW = 2


def from_behind(value, axis, steps):
    count = lax.axis_size(axis)
    pairs = [(source, (source + steps) % count) for source in range(count)]
    return lax.ppermute(value, axis, pairs)


def pair_table(levels):
    return [
        (target_lvl, source_lvl)
        for target_lvl in range(1, levels)
        for source_lvl in range(target_lvl)
    ]


def offset_choices(window, count):
    values = sorted(set(list(range(window)) + [count // 2, count - 1]))
    return values


def offset_places(offsets, values):
    places = jnp.zeros(offsets.shape, jnp.int32)
    for position, value in enumerate(values):
        places = places + jnp.where(offsets == value, position, 0).astype(jnp.int32)
    return places


def spread_rows(indices, row_count, products):
    onehot = (indices[None, :] == jnp.arange(row_count, dtype=jnp.int32)[:, None]).astype(
        jnp.float32
    )
    flattened = products.reshape(products.shape[0], -1)
    summed = jnp.dot(
        onehot, flattened, precision=lax.Precision.HIGHEST, preferred_element_type=jnp.float32
    )
    return summed.reshape((row_count,) + products.shape[1:])


def deliver_rows(partial_value, values):
    summed = partial_value[0].astype(jnp.bfloat16).astype(jnp.float32)
    for position in range(1, partial_value.shape[0]):
        moved = from_behind(partial_value[position].astype(jnp.bfloat16), "row", values[position])
        summed = summed + moved.astype(jnp.float32)
    return summed


def deliver_cols(partial_value, values):
    summed = partial_value[0].astype(jnp.bfloat16).astype(jnp.float32)
    for position in range(1, partial_value.shape[0]):
        moved = from_behind(partial_value[position].astype(jnp.bfloat16), "col", values[position])
        summed = summed + moved.astype(jnp.float32)
    return summed


def shards(rhs_panels, inverse_diag, factor_blocks, block_target, block_source):
    levels = rhs_panels.shape[0]
    row_devices = lax.axis_size("row")
    col_devices = lax.axis_size("col")
    pair_list = pair_table(levels)
    blocks = factor_blocks[:, 0]
    targets = block_target[:, 0]
    sources = block_source[:, 0]
    row_values = offset_choices(WINDOW, row_devices)
    col_values = offset_choices(WINDOW, col_devices)
    row_keys = offset_places((targets - lax.axis_index("row")) % row_devices, row_values)
    col_keys = offset_places((sources - lax.axis_index("col")) % col_devices, col_values)
    row_width = len(row_values)
    col_width = len(col_values)
    forward = []
    gathered = {}
    for current in range(levels):
        residual = rhs_panels[current, 0, 0]
        if current > 0:
            partial_value = jnp.zeros((row_width,) + residual.shape, jnp.float32)
            for pair_idx, pair_info in enumerate(pair_list):
                if pair_info[0] == current:
                    picked = jnp.take(gathered[pair_info[1]], sources[pair_idx], axis=0)
                    products = jnp.einsum(
                        "snb,sab->sna", picked, blocks[pair_idx], preferred_element_type=jnp.float32
                    )
                    partial_value = partial_value + spread_rows(
                        row_keys[pair_idx], row_width, products
                    )
            summed = deliver_rows(partial_value, row_values)
            residual = residual - summed
        reduced = residual.astype(jnp.bfloat16)
        panel_now = lax.dot_general(
            reduced,
            inverse_diag[current, 0, 0],
            (((1,), (1,)), ((), ())),
            preferred_element_type=jnp.float32,
        )
        forward.append(panel_now)
        if current < levels - 1:
            outgoing = panel_now.astype(jnp.bfloat16)[None]
            gathered[current] = lax.all_gather(outgoing, "col", axis=0, tiled=True)
    solutions = [None] * levels
    gathered_back = {}
    for current in reversed(range(levels)):
        residual = forward[current]
        if current < levels - 1:
            partial_value = jnp.zeros((col_width,) + residual.shape, jnp.float32)
            for pair_idx, pair_info in enumerate(pair_list):
                if pair_info[1] == current:
                    picked = jnp.take(gathered_back[pair_info[0]], targets[pair_idx], axis=0)
                    products = jnp.einsum(
                        "snb,sba->sna", picked, blocks[pair_idx], preferred_element_type=jnp.float32
                    )
                    partial_value = partial_value + spread_rows(
                        col_keys[pair_idx], col_width, products
                    )
            summed = deliver_cols(partial_value, col_values)
            residual = residual - summed
        reduced = residual.astype(jnp.bfloat16)
        answer = jnp.dot(reduced, inverse_diag[current, 0, 0], preferred_element_type=jnp.float32)
        solutions[current] = answer
        if current > 0:
            outgoing = answer.astype(jnp.bfloat16)[None]
            gathered_back[current] = lax.all_gather(outgoing, "row", axis=0, tiled=True)
    return jnp.stack(solutions)[:, None, None]


def solution(mesh):
    placed = (
        P(None, "row", "col", None, None),
        P(None, "row", "col", None, None),
        P(None, "row", "col", None, None),
        P(None, "row", "col"),
        P(None, "row", "col"),
    )
    return jax.shard_map(
        shards,
        mesh=mesh,
        in_specs=placed,
        out_specs=P(None, "row", "col", None, None),
        check_vma=False,
    )
```

profile of v0, /device:TPU:0, one launch (start us, length us, event | category | flops | bytes accessed | tf_op | source)
XLA Modules:
  0.0 95.2 jit_solution(5087454735423842611)
XLA Ops:
  0.0 1.1 %fusion.101 = (bf16[64,256]{1,0:T(8,128)(2,1)S(1)}, f32[64,256]{1,0:T(8,128)S(1)}) fusion(bf16[3,1,1,256,256]{4,3,2,1,0:T(8,128)(2,1)} %param.10, f32[3,1,1,64,256]{4,3,2,1,0:T(8,128)} %param.9), kind=kOutput, calls=%fused_computation.168 | convolution fusion | flops 8404992 | bytes 262144 | tf_op jit(solution)/shard_map/dot_general | solution.py:94
  1.1 10.8 %all-gather = bf16[512,256]{1,0:T(8,128)(2,1)S(1)} all-gather(bf16[64,256]{1,0:T(8,128)(2,1)S(1)} %get-tuple-element.46), channel_id=2, replica_groups=mesh['row'=4,'col'=8] {'col'}, dimensions={0}, use_global_device_ids=true | all-gather | bytes 294912 | tf_op jit(solution)/shard_map/all_gather | solution.py:103
  13.9 1.8 %fusion.10 = f32[10,64,256]{2,1,0:T(8,128)S(1)} fusion(bf16[3,1,10,256,256]{4,3,2,1,0:T(8,128)(2,1)} %param.11, bf16[10,64,256]{2,1,0:T(8,128)(2,1)S(1)} %gather_fusion, pred[10]{0:T(512)(128)(4,1)S(1)} %get-tuple-element.42), kind=kOutput, calls=%fused_computation.18 | convolution fusion | flops 84049920 | bytes 2293770 | tf_op jit(solution)/shard_map/snb,sab->sna/dot_general | solution.py:85
  17.6 3.7 %collective-permute-start.2 = (bf16[64,256]{1,0:T(8,128)(2,1)S(1)}, bf16[64,256]{1,0:T(8,128)(2,1)S(1)}, u32[]{:S(2)}, u32[]{:S(2)}) collective-permute-start(bf16[64,256]{1,0:T(8,128)(2,1)S(1)} %convert_element_type.161), channel_id=1, source_target_pairs={{0,24},{8,0},{16,8},{24,16},{1,25},{9,1},{17,9},{25,17},{2,26},{10... | collective-permute-start | bytes 98312 | tf_op jit(solution)/shard_map/ppermute | solution.py:12
  21.3 1.1 %collective-permute-start = (bf16[64,256]{1,0:T(8,128)(2,1)S(1)}, bf16[64,256]{1,0:T(8,128)(2,1)S(1)}, u32[]{:S(2)}, u32[]{:S(2)}) collective-permute-start(bf16[64,256]{1,0:T(8,128)(2,1)S(1)} %convert_element_type.157), channel_id=1, source_target_pairs={{0,8},{8,16},{16,24},{24,0},{1,9},{9,17},{17,25},{25,1},{2,10},{10... | collective-permute-start | bytes 98312 | tf_op jit(solution)/shard_map/ppermute | solution.py:12
  23.2 1.8 %fusion.6 = f32[10,64,256]{2,1,0:T(8,128)S(1)} fusion(bf16[3,1,10,256,256]{4,3,2,1,0:T(8,128)(2,1)} %param.11, bf16[10,64,256]{2,1,0:T(8,128)(2,1)S(1)} %gather_fusion.1, pred[10]{0:T(512)(128)(4,1)S(1)} %get-tuple-element.44), kind=kOutput, calls=%fused_computation.14 | convolution fusion | flops 84049920 | bytes 2293770 | tf_op jit(solution)/shard_map/snb,sab->sna/dot_general | solution.py:85
  25.1 0.8 fusion.25
  27.3 9.3 %all-gather.1 = bf16[512,256]{1,0:T(8,128)(2,1)S(1)} all-gather(bf16[64,256]{1,0:T(8,128)(2,1)S(1)} %get-tuple-element.48), channel_id=3, replica_groups=mesh['row'=4,'col'=8] {'col'}, dimensions={0}, use_global_device_ids=true | all-gather | bytes 294912 | tf_op jit(solution)/shard_map/all_gather | solution.py:103
  37.1 1.8 %fusion.2 = f32[10,64,256]{2,1,0:T(8,128)S(1)} fusion(bf16[3,1,10,256,256]{4,3,2,1,0:T(8,128)(2,1)} %param.11, bf16[10,64,256]{2,1,0:T(8,128)(2,1)S(1)} %gather_fusion.2, pred[10]{0:T(512)(128)(4,1)S(1)} %get-tuple-element.19), kind=kOutput, calls=%fused_computation.10 | convolution fusion | flops 84049920 | bytes 2293770 | tf_op jit(solution)/shard_map/snb,sab->sna/dot_general | solution.py:85
  39.0 0.8 fusion.18
  40.1 1.8 %collective-permute-start.5 = (bf16[64,256]{1,0:T(8,128)(2,1)S(1)}, bf16[64,256]{1,0:T(8,128)(2,1)S(1)}, u32[]{:S(2)}, u32[]{:S(2)}) collective-permute-start(bf16[64,256]{1,0:T(8,128)(2,1)S(1)} %bitcast.222), channel_id=1, source_target_pairs={{0,24},{8,0},{16,8},{24,16},{1,25},{9,1},{17,9},{25,17},{2,26},{10... | collective-permute-start | bytes 98312 | tf_op jit(solution)/shard_map/ppermute | solution.py:12
  41.9 1.1 %collective-permute-start.4 = (bf16[64,256]{1,0:T(8,128)(2,1)S(1)}, bf16[64,256]{1,0:T(8,128)(2,1)S(1)}, u32[]{:S(2)}, u32[]{:S(2)}) collective-permute-start(bf16[64,256]{1,0:T(8,128)(2,1)S(1)} %bitcast.223), channel_id=1, source_target_pairs={{0,16},{8,24},{16,0},{24,8},{1,17},{9,25},{17,1},{25,9},{2,18},{10... | collective-permute-start | bytes 98312 | tf_op jit(solution)/shard_map/ppermute | solution.py:12
  44.0 2.7 %collective-permute-done.4 = bf16[64,256]{1,0:T(8,128)(2,1)S(1)} collective-permute-done((bf16[64,256]{1,0:T(8,128)(2,1)S(1)}, bf16[64,256]{1,0:T(8,128)(2,1)S(1)}, u32[]{:S(2)}, u32[]{:S(2)}) %collective-permute-start.4) | collective-permute-done | bytes 32800 | tf_op jit(solution)/shard_map/ppermute | solution.py:12
  46.8 2.0 %collective-permute-done.3 = bf16[64,256]{1,0:T(8,128)(2,1)S(1)} collective-permute-done((bf16[64,256]{1,0:T(8,128)(2,1)S(1)}, bf16[64,256]{1,0:T(8,128)(2,1)S(1)}, u32[]{:S(2)}, u32[]{:S(2)}) %collective-permute-start.3) | collective-permute-done | bytes 32800 | tf_op jit(solution)/shard_map/ppermute | solution.py:12
  49.0 13.4 %all-gather.2 = bf16[256,256]{1,0:T(8,128)(2,1)S(1)} all-gather(bf16[64,256]{1,0:T(8,128)(2,1)S(1)} %get-tuple-element.50), channel_id=4, replica_groups=mesh['row'=4,'col'=8] {'row'}, dimensions={0}, use_global_device_ids=true | all-gather | bytes 163840 | tf_op jit(solution)/shard_map/all_gather | solution.py:126
  63.0 1.7 %fusion = f32[10,64,256]{2,1,0:T(8,128)S(1)} fusion(bf16[3,1,10,256,256]{4,3,2,1,0:T(8,128)(2,1)} %param.11, bf16[10,64,256]{2,1,0:T(8,128)(2,1)S(1)} %gather_fusion.3, pred[10]{0:T(512)(128)(4,1)S(1)} %get-tuple-element.38), kind=kOutput, calls=%fused_computation.8 | convolution fusion | flops 84049920 | bytes 2293770 | tf_op jit(solution)/shard_map/snb,sba->sna/dot_general | solution.py:113
  68.0 1.7 %fusion.4 = f32[10,64,256]{2,1,0:T(8,128)S(1)} fusion(bf16[3,1,10,256,256]{4,3,2,1,0:T(8,128)(2,1)} %param.11, bf16[10,64,256]{2,1,0:T(8,128)(2,1)S(1)} %gather_fusion.5, pred[10]{0:T(512)(128)(4,1)S(1)} %get-tuple-element.40), kind=kOutput, calls=%fused_computation.12 | convolution fusion | flops 84049920 | bytes 2293770 | tf_op jit(solution)/shard_map/snb,sba->sna/dot_general | solution.py:113
  69.8 0.8 fusion.20
  71.6 13.6 %all-gather.3 = bf16[256,256]{1,0:T(8,128)(2,1)S(1)} all-gather(bf16[64,256]{1,0:T(8,128)(2,1)S(1)} %get-tuple-element.52), channel_id=5, replica_groups=mesh['row'=4,'col'=8] {'row'}, dimensions={0}, use_global_device_ids=true | all-gather | bytes 163840 | tf_op jit(solution)/shard_map/all_gather | solution.py:126
  85.8 1.7 %fusion.8 = f32[10,64,256]{2,1,0:T(8,128)S(1)} fusion(bf16[3,1,10,256,256]{4,3,2,1,0:T(8,128)(2,1)} %param.11, bf16[10,64,256]{2,1,0:T(8,128)(2,1)S(1)} %gather_fusion.4, pred[10]{0:T(512)(128)(4,1)S(1)} %get-tuple-element.13), kind=kOutput, calls=%fused_computation.16 | convolution fusion | flops 84049920 | bytes 2293770 | tf_op jit(solution)/shard_map/snb,sba->sna/dot_general | solution.py:113
  87.6 0.8 fusion.22
  88.6 1.5 %collective-permute-start.10 = (bf16[64,256]{1,0:T(8,128)(2,1)S(1)}, bf16[64,256]{1,0:T(8,128)(2,1)S(1)}, u32[]{:S(2)}, u32[]{:S(2)}) collective-permute-start(bf16[64,256]{1,0:T(8,128)(2,1)S(1)} %get-tuple-element.27), channel_id=1, source_target_pairs={{0,4},{1,5},{2,6},{3,7},{4,0},{5,1},{6,2},{7,3},{8,12},{9,13},{10,... | collective-permute-start | bytes 98312 | tf_op jit(solution)/shard_map/ppermute | solution.py:12
  90.3 2.3 %collective-permute-done.10 = bf16[64,256]{1,0:T(8,128)(2,1)S(1)} collective-permute-done((bf16[64,256]{1,0:T(8,128)(2,1)S(1)}, bf16[64,256]{1,0:T(8,128)(2,1)S(1)}, u32[]{:S(2)}, u32[]{:S(2)}) %collective-permute-start.10) | collective-permute-done | bytes 32800 | tf_op jit(solution)/shard_map/ppermute | solution.py:12
  92.6 1.8 %collective-permute-done.9 = bf16[64,256]{1,0:T(8,128)(2,1)S(1)} collective-permute-done((bf16[64,256]{1,0:T(8,128)(2,1)S(1)}, bf16[64,256]{1,0:T(8,128)(2,1)S(1)}, u32[]{:S(2)}, u32[]{:S(2)}) %collective-permute-start.9) | collective-permute-done | bytes 32800 | tf_op jit(solution)/shard_map/ppermute | solution.py:12
  (74 shorter events, 14.7 us)
Async XLA Ops:
  13.9 8.7 %copy-start.2 = (s32[3,1,10]{2,1,0:T(1,128)S(1)}, s32[3,1,10]{2,1,0:T(1,128)}, u32[]{:S(2)}) copy-start(s32[3,1,10]{2,1,0:T(1,128)} %param.12) | copy-start | bytes 364
  15.8 9.2 %copy-start.3 = (s32[3,1,10]{2,1,0:T(1,128)S(1)}, s32[3,1,10]{2,1,0:T(1,128)}, u32[]{:S(2)}) copy-start(s32[3,1,10]{2,1,0:T(1,128)} %param.13) | copy-start | bytes 364
  16.5 10.6 %copy-start = (bf16[3,1,1,256,256]{4,3,2,1,0:T(8,128)(2,1)S(1)}, bf16[3,1,1,256,256]{4,3,2,1,0:T(8,128)(2,1)}, u32[]{:S(2)}) copy-start(bf16[3,1,1,256,256]{4,3,2,1,0:T(8,128)(2,1)} %param.10) | copy-start | bytes 1179652
  16.5 10.6 %copy-start.1 = (f32[3,1,1,64,256]{4,3,2,1,0:T(8,128)S(1)}, f32[3,1,1,64,256]{4,3,2,1,0:T(8,128)}, u32[]{:S(2)}) copy-start(f32[3,1,1,64,256]{4,3,2,1,0:T(8,128)} %param.9) | copy-start | bytes 589828
  17.6 8.4 %collective-permute-start.2 = (bf16[64,256]{1,0:T(8,128)(2,1)S(1)}, bf16[64,256]{1,0:T(8,128)(2,1)S(1)}, u32[]{:S(2)}, u32[]{:S(2)}) collective-permute-start(bf16[64,256]{1,0:T(8,128)(2,1)S(1)} %convert_element_type.161), channel_id=1, source_target_pairs={{0,24},{8,0},{16,8},{24,16},{1,25},{9,1},{17,9},{25,17},{2,26},{10... | collective-permute-start | bytes 98312 | tf_op jit(solution)/shard_map/ppermute | solution.py:12
  21.2 5.2 %collective-permute-start.1 = (bf16[64,256]{1,0:T(8,128)(2,1)S(1)}, bf16[64,256]{1,0:T(8,128)(2,1)S(1)}, u32[]{:S(2)}, u32[]{:S(2)}) collective-permute-start(bf16[64,256]{1,0:T(8,128)(2,1)S(1)} %convert_element_type.159), channel_id=1, source_target_pairs={{0,16},{8,24},{16,0},{24,8},{1,17},{9,25},{17,1},{25,9},{2,18},{10... | collective-permute-start | bytes 98312 | tf_op jit(solution)/shard_map/ppermute | solution.py:12
  21.3 5.8 %collective-permute-start = (bf16[64,256]{1,0:T(8,128)(2,1)S(1)}, bf16[64,256]{1,0:T(8,128)(2,1)S(1)}, u32[]{:S(2)}, u32[]{:S(2)}) collective-permute-start(bf16[64,256]{1,0:T(8,128)(2,1)S(1)} %convert_element_type.157), channel_id=1, source_target_pairs={{0,8},{8,16},{16,24},{24,0},{1,9},{9,17},{17,25},{25,1},{2,10},{10... | collective-permute-start | bytes 98312 | tf_op jit(solution)/shard_map/ppermute | solution.py:12
  40.1 4.0 %collective-permute-start.5 = (bf16[64,256]{1,0:T(8,128)(2,1)S(1)}, bf16[64,256]{1,0:T(8,128)(2,1)S(1)}, u32[]{:S(2)}, u32[]{:S(2)}) collective-permute-start(bf16[64,256]{1,0:T(8,128)(2,1)S(1)} %bitcast.222), channel_id=1, source_target_pairs={{0,24},{8,0},{16,8},{24,16},{1,25},{9,1},{17,9},{25,17},{2,26},{10... | collective-permute-start | bytes 98312 | tf_op jit(solution)/shard_map/ppermute | solution.py:12
  41.9 4.9 %collective-permute-start.4 = (bf16[64,256]{1,0:T(8,128)(2,1)S(1)}, bf16[64,256]{1,0:T(8,128)(2,1)S(1)}, u32[]{:S(2)}, u32[]{:S(2)}) collective-permute-start(bf16[64,256]{1,0:T(8,128)(2,1)S(1)} %bitcast.223), channel_id=1, source_target_pairs={{0,16},{8,24},{16,0},{24,8},{1,17},{9,25},{17,1},{25,9},{2,18},{10... | collective-permute-start | bytes 98312 | tf_op jit(solution)/shard_map/ppermute | solution.py:12
  43.0 5.7 %collective-permute-start.3 = (bf16[64,256]{1,0:T(8,128)(2,1)S(1)}, bf16[64,256]{1,0:T(8,128)(2,1)S(1)}, u32[]{:S(2)}, u32[]{:S(2)}) collective-permute-start(bf16[64,256]{1,0:T(8,128)(2,1)S(1)} %bitcast.224), channel_id=1, source_target_pairs={{0,8},{8,16},{16,24},{24,0},{1,9},{9,17},{17,25},{25,1},{2,10},{10... | collective-permute-start | bytes 98312 | tf_op jit(solution)/shard_map/ppermute | solution.py:12
  66.5 4.3 %collective-permute-start.8 = (bf16[64,256]{1,0:T(8,128)(2,1)S(1)}, bf16[64,256]{1,0:T(8,128)(2,1)S(1)}, u32[]{:S(2)}, u32[]{:S(2)}) collective-permute-start(bf16[64,256]{1,0:T(8,128)(2,1)S(1)} %convert_element_type.182), channel_id=1, source_target_pairs={{0,7},{1,0},{2,1},{3,2},{4,3},{5,4},{6,5},{7,6},{8,15},{9,8},{10,9... | collective-permute-start | bytes 98312 | tf_op jit(solution)/shard_map/ppermute | solution.py:12
  66.6 4.3 %collective-permute-start.7 = (bf16[64,256]{1,0:T(8,128)(2,1)S(1)}, bf16[64,256]{1,0:T(8,128)(2,1)S(1)}, u32[]{:S(2)}, u32[]{:S(2)}) collective-permute-start(bf16[64,256]{1,0:T(8,128)(2,1)S(1)} %convert_element_type.180), channel_id=1, source_target_pairs={{0,4},{1,5},{2,6},{3,7},{4,0},{5,1},{6,2},{7,3},{8,12},{9,13},{10,... | collective-permute-start | bytes 98312 | tf_op jit(solution)/shard_map/ppermute | solution.py:12
  67.2 4.3 %collective-permute-start.6 = (bf16[64,256]{1,0:T(8,128)(2,1)S(1)}, bf16[64,256]{1,0:T(8,128)(2,1)S(1)}, u32[]{:S(2)}, u32[]{:S(2)}) collective-permute-start(bf16[64,256]{1,0:T(8,128)(2,1)S(1)} %convert_element_type.178), channel_id=1, source_target_pairs={{0,1},{1,2},{2,3},{3,4},{4,5},{5,6},{6,7},{7,0},{8,9},{9,10},{10,1... | collective-permute-start | bytes 98312 | tf_op jit(solution)/shard_map/ppermute | solution.py:12
  88.5 1.7 %collective-permute-start.11 = (bf16[64,256]{1,0:T(8,128)(2,1)S(1)}, bf16[64,256]{1,0:T(8,128)(2,1)S(1)}, u32[]{:S(2)}, u32[]{:S(2)}) collective-permute-start(bf16[64,256]{1,0:T(8,128)(2,1)S(1)} %get-tuple-element.26), channel_id=1, source_target_pairs={{0,7},{1,0},{2,1},{3,2},{4,3},{5,4},{6,5},{7,6},{8,15},{9,8},{10,9... | collective-permute-start | bytes 98312 | tf_op jit(solution)/shard_map/ppermute | solution.py:12
  88.6 4.0 %collective-permute-start.10 = (bf16[64,256]{1,0:T(8,128)(2,1)S(1)}, bf16[64,256]{1,0:T(8,128)(2,1)S(1)}, u32[]{:S(2)}, u32[]{:S(2)}) collective-permute-start(bf16[64,256]{1,0:T(8,128)(2,1)S(1)} %get-tuple-element.27), channel_id=1, source_target_pairs={{0,4},{1,5},{2,6},{3,7},{4,0},{5,1},{6,2},{7,3},{8,12},{9,13},{10,... | collective-permute-start | bytes 98312 | tf_op jit(solution)/shard_map/ppermute | solution.py:12
  90.1 4.2 %collective-permute-start.9 = (bf16[64,256]{1,0:T(8,128)(2,1)S(1)}, bf16[64,256]{1,0:T(8,128)(2,1)S(1)}, u32[]{:S(2)}, u32[]{:S(2)}) collective-permute-start(bf16[64,256]{1,0:T(8,128)(2,1)S(1)} %get-tuple-element.25), channel_id=1, source_target_pairs={{0,1},{1,2},{2,3},{3,4},{4,5},{5,6},{6,7},{7,0},{8,9},{9,10},{10,1... | collective-permute-start | bytes 98312 | tf_op jit(solution)/shard_map/ppermute | solution.py:12
where the time goes:
time: 95.6 us; the launch traced here: 95.2 us
  blocking collectives  47.1 us (49%)
  matrix products  16.7 us (17%)
  waiting for transfers between devices  11.3 us (12%)
  starting transfers between devices  10.6 us (11%)
  local copies, waits for them, and re-layouts  6.29 us (7%)
  other arithmetic  2.76 us (3%)
    all_gather x2, blocking collectives, shards(): gathered_back[current] = lax.all_gather(outgoing, 'row', axis=0, tiled=True)  27 us
    all_gather x2, blocking collectives, shards(): gathered[current] = lax.all_gather(outgoing, 'col', axis=0, tiled=True)  20.1 us
    ppermute x12, waiting for transfers between devices, from_behind(): return lax.ppermute(value, axis, pairs)  11.3 us
    ppermute x12, starting transfers between devices, from_behind(): return lax.ppermute(value, axis, pairs)  10.6 us
    dot_general x3, matrix products, shards(): jnp.einsum('snb,sab->sna', picked, blocks[pair_idx], preferred_element_ty...  5.52 us
    dot_general x3, matrix products, shards(): jnp.einsum('snb,sba->sna', picked, blocks[pair_idx], preferred_element_ty...  5.14 us
    dot_general x6, matrix products, spread_rows(): jnp.dot(onehot, flattened, precision=lax.Precision.HIGHEST, preferred_ele...  4.18 us
  transfers between devices with their start and end apart: 12, of which 8 were waited for; matrix products, arithmetic and copies ran while one was open for 7% of the time, Pallas kernels for 0%

commit v1 on v0

v1 whole, which is shorter than its diff:
```python
import functools

import jax
import jax.numpy as jnp
from jax import lax
from jax.experimental import pallas as pl
from jax.experimental.pallas import tpu as pltpu
from jax.sharding import PartitionSpec as P

WINDOW = 2
MESH = pl.DeviceIdType.MESH


def pair_table(levels):
    return [(d, s) for d in range(1, levels) for s in range(d)]


def offset_choices(window, count):
    return sorted(set(list(range(window)) + [count // 2, count - 1]))


def kernel(
    n_row,
    n_col,
    rhs_hbm,
    inv_hbm,
    fac_hbm,
    tgt_ref,
    src_ref,
    out_ref,
    rhs,
    inv,
    fac,
    ycol,
    brow,
    fpart,
    frecv,
    bpart,
    brecv,
    yfull,
    facc,
    bacc,
    ftab,
    btab,
    rhs_sem,
    inv_sem,
    fac_sem,
    send_sem,
    recv_sem,
):
    levels = rhs.shape[0]
    slots = fac.shape[1]
    nrhs = rhs.shape[1]
    pairs = pair_table(levels)
    row_vals = offset_choices(WINDOW, n_row)
    col_vals = offset_choices(WINDOW, n_col)
    row_w, col_w = len(row_vals), len(col_vals)
    me_r, me_c = lax.axis_index("row"), lax.axis_index("col")

    def row_dev(steps):
        return {"row": lax.rem(me_r + (steps + n_row), n_row)}

    def col_dev(steps):
        return {"col": lax.rem(me_c + (steps + n_col), n_col)}

    loads = {}
    for k in range(levels):
        loads["rhs", k] = pltpu.make_async_copy(rhs_hbm.at[k, 0, 0], rhs.at[k], rhs_sem.at[k])
        loads["inv", k] = pltpu.make_async_copy(inv_hbm.at[k, 0, 0], inv.at[k], inv_sem.at[k])
    for p in range(len(pairs)):
        loads["fac", p] = pltpu.make_async_copy(fac_hbm.at[p, 0], fac.at[p], fac_sem.at[p])
    loads["rhs", 0].start()
    loads["inv", 0].start()
    loads["fac", 0].start()
    for k in range(1, levels):
        loads["rhs", k].start()
        loads["inv", k].start()
    for p in range(1, len(pairs)):
        loads["fac", p].start()
    loaded = set()

    def need(*key):
        if key not in loaded:
            loads[key].wait()
            loaded.add(key)

    barrier = pltpu.get_barrier_semaphore()
    for v in row_vals[1:]:
        pl.semaphore_signal(barrier, inc=1, device_id=row_dev(v), device_id_type=MESH)
    for v in col_vals[1:]:
        pl.semaphore_signal(barrier, inc=1, device_id=col_dev(v), device_id_type=MESH)

    sends = []

    def send(phase, slot, src, dst, device):
        copy = pltpu.make_async_remote_copy(
            src_ref=src,
            dst_ref=dst,
            send_sem=send_sem.at[phase, slot],
            recv_sem=recv_sem.at[phase, slot],
            device_id=device,
            device_id_type=MESH,
        )
        copy.start()
        sends.append(copy)
        return copy

    def dot_t(a, b):
        return lax.dot_general(a, b, (((1,), (1,)), ((), ())), preferred_element_type=jnp.float32)

    def dot_n(a, b):
        return jnp.dot(a, b, preferred_element_type=jnp.float32)

    def order(vals):
        return [k for k in (2, 3, 1) if k < len(vals)] + list(range(4, len(vals)))

    def product(p, panels, table, width, dot):
        need("fac", p)
        total = None
        for q in range(slots):
            stacked = jnp.concatenate([panels[table[p, q, j]] for j in range(width)], axis=0)
            term = dot(stacked, fac[p, q])
            total = term if total is None else total + term
        return total

    def spread(phase, vals, device, total, part, recv):
        copies = []
        for k in order(vals):
            part[k] = total[k * nrhs : (k + 1) * nrhs].astype(jnp.bfloat16)
            copies.append(send(phase, k, part.at[k], recv.at[k], device(vals[k])))
        return copies, total[:nrhs].astype(jnp.bfloat16).astype(jnp.float32)

    def collect(copies, recv, own, width):
        for copy in copies:
            copy.wait_recv()
        for k in range(1, width):
            own = own + recv[k].astype(jnp.float32)
        return own

    def share(phase, vals, device, panels):
        return [
            send(phase, k, panels.at[0], panels.at[k], device(-vals[k])) for k in order(vals)
        ]

    need("rhs", 0)
    need("inv", 0)
    y = dot_t(rhs[0].astype(jnp.bfloat16), inv[0])
    yfull[0] = y
    ycol[0][0] = y.astype(jnp.bfloat16)
    pl.semaphore_wait(barrier, row_w + col_w - 2)
    phase = 0
    copies = share(phase, col_vals, col_dev, ycol[0])

    for lvl in range(levels - 1):
        ycol[lvl][col_w] = jnp.zeros((nrhs, rhs.shape[2]), jnp.bfloat16)
        brow[lvl + 1][row_w] = jnp.zeros((nrhs, rhs.shape[2]), jnp.bfloat16)
    for p in range(len(pairs)):
        for q in range(slots):
            off_r = tgt_ref[p, 0, q] - me_r
            off_c = src_ref[p, 0, q] - me_c
            off_r = jnp.where(off_r < 0, off_r + n_row, off_r)
            off_c = jnp.where(off_c < 0, off_c + n_col, off_c)
            pos_r = jnp.int32(0)
            for k in range(1, row_w):
                pos_r = jnp.where(off_r == row_vals[k], k, pos_r)
            pos_c = jnp.int32(0)
            for k in range(1, col_w):
                pos_c = jnp.where(off_c == col_vals[k], k, pos_c)
            for k in range(row_w):
                ftab[p, q, k] = jnp.where(pos_r == k, pos_c, col_w)
            for k in range(col_w):
                btab[p, q, k] = jnp.where(pos_c == k, pos_r, row_w)

    for k in range(1, levels):
        total = None
        for p, (d, s) in enumerate(pairs):
            if d == k and s == k - 1:
                for copy in copies:
                    copy.wait_recv()
                total = product(p, ycol[s], ftab, row_w, dot_t)
        if k > 1:
            total = total + facc[k]
        phase += 1
        copies, own = spread(phase, row_vals, row_dev, total, fpart.at[k], frecv.at[k])
        for p, (d, s) in enumerate(pairs):
            if s == k - 1 and d > k:
                later = product(p, ycol[s], ftab, row_w, dot_t)
                facc[d] = later if s == 0 else facc[d] + later
        need("rhs", k)
        need("inv", k)
        fsum = collect(copies, frecv.at[k], own, row_w)
        y = dot_t((rhs[k] - fsum).astype(jnp.bfloat16), inv[k])
        if k < levels - 1:
            yfull[k] = y
            ycol[k][0] = y.astype(jnp.bfloat16)
            phase += 1
            copies = share(phase, col_vals, col_dev, ycol[k])

    top = levels - 1
    answer = dot_n(y.astype(jnp.bfloat16), inv[top])
    brow[top][0] = answer.astype(jnp.bfloat16)
    phase += 1
    copies = share(phase, row_vals, row_dev, brow[top])
    out_ref[top, 0, 0] = answer
    for k in reversed(range(top)):
        total = None
        for p, (d, s) in enumerate(pairs):
            if s == k and d == k + 1:
                for copy in copies:
                    copy.wait_recv()
                total = product(p, brow[d], btab, col_w, dot_n)
        if k + 1 < top:
            total = total + bacc[k]
        phase += 1
        copies, own = spread(phase, col_vals, col_dev, total, bpart.at[k], brecv.at[k])
        for p, (d, s) in enumerate(pairs):
            if d == k + 1 and s < k:
                later = product(p, brow[d], btab, col_w, dot_n)
                bacc[s] = later if d == top else bacc[s] + later
        bsum = collect(copies, brecv.at[k], own, col_w)
        answer = dot_n((yfull[k] - bsum).astype(jnp.bfloat16), inv[k])
        if k > 0:
            brow[k][0] = answer.astype(jnp.bfloat16)
            phase += 1
            copies = share(phase, row_vals, row_dev, brow[k])
        out_ref[k, 0, 0] = answer
    for copy in sends:
        copy.wait_send()


def shards(n_row, n_col, rhs, inv, fac, tgt, src):
    levels, nrhs, size = rhs.shape[0], rhs.shape[3], rhs.shape[4]
    pairs, slots = fac.shape[0], fac.shape[2]
    row_w = len(offset_choices(WINDOW, n_row))
    col_w = len(offset_choices(WINDOW, n_col))
    width = max(row_w, col_w)
    phases = 4 * (levels - 1)
    bf, f32 = jnp.bfloat16, jnp.float32
    return pl.pallas_call(
        functools.partial(kernel, n_row, n_col),
        out_shape=jax.ShapeDtypeStruct(rhs.shape, f32),
        in_specs=[pl.BlockSpec(memory_space=pl.ANY)] * 3
        + [pl.BlockSpec(memory_space=pltpu.SMEM)] * 2,
        out_specs=pl.BlockSpec(memory_space=pltpu.VMEM),
        scratch_shapes=[
            pltpu.VMEM((levels, nrhs, size), f32),
            pltpu.VMEM((levels, size, size), bf),
            pltpu.VMEM((pairs, slots, size, size), bf),
            [pltpu.VMEM((col_w + 1, nrhs, size), bf)] * (levels - 1),
            [pltpu.VMEM((row_w + 1, nrhs, size), bf)] * levels,
            pltpu.VMEM((levels, row_w, nrhs, size), bf),
            pltpu.VMEM((levels, row_w, nrhs, size), bf),
            pltpu.VMEM((levels - 1, col_w, nrhs, size), bf),
            pltpu.VMEM((levels - 1, col_w, nrhs, size), bf),
            pltpu.VMEM((levels - 1, nrhs, size), f32),
            pltpu.VMEM((levels, row_w * nrhs, size), f32),
            pltpu.VMEM((levels - 1, col_w * nrhs, size), f32),
            pltpu.SMEM((pairs, slots, row_w), jnp.int32),
            pltpu.SMEM((pairs, slots, col_w), jnp.int32),
            pltpu.SemaphoreType.DMA((levels,)),
            pltpu.SemaphoreType.DMA((levels,)),
            pltpu.SemaphoreType.DMA((pairs,)),
            pltpu.SemaphoreType.DMA((phases, width)),
            pltpu.SemaphoreType.DMA((phases, width)),
        ],
        compiler_params=pltpu.CompilerParams(collective_id=0, has_side_effects=True),
    )(rhs, inv, fac, tgt, src)


def solution(mesh):
    placed = (
        P(None, "row", "col", None, None),
        P(None, "row", "col", None, None),
        P(None, "row", "col", None, None),
        P(None, "row", "col"),
        P(None, "row", "col"),
    )
    return jax.shard_map(
        functools.partial(shards, mesh.shape["row"], mesh.shape["col"]),
        mesh=mesh,
        in_specs=placed,
        out_specs=P(None, "row", "col", None, None),
        check_vma=False,
    )
```

time: 95.6 us -> 44.1 us (0.46)
  blocking collectives: 47.1 us -> 0 us
  Pallas kernels: 0 us -> 42.3 us
  matrix products: 16.7 us -> 0 us
  waiting for transfers between devices: 11.3 us -> 0 us
  starting transfers between devices: 10.6 us -> 0 us
  local copies, waits for them, and re-layouts: 6.29 us -> 1.62 us
  other arithmetic: 2.76 us -> 0 us
    all_gather x4 -> x0, blocking collectives: 47.1 us -> none  [the longest x2 27 us: shards(): gathered_back[current] = lax.all_gather(outgoing, 'row', axis=0, tiled=True)]
    pallas_call x0 -> x1, Pallas kernels: none -> 42.3 us  [shards(): pl.pallas_call(functools.partial(kernel, n_row, n_col), out_shape=jax.Sha...]
    dot_general x17 -> x0, matrix products: 16.7 us -> none  [the longest x3 5.52 us: shards(): jnp.einsum('snb,sab->sna', picked, blocks[pair_idx], preferred_element_ty...]
    ppermute x12 -> x0, waiting for transfers between devices: 11.3 us -> none  [from_behind(): return lax.ppermute(value, axis, pairs)]
    ppermute x12 -> x0, starting transfers between devices: 10.6 us -> none  [from_behind(): return lax.ppermute(value, axis, pairs)]
    gather x6 -> x0, local copies, waits for them, and re-layouts: 3.4 us -> none  [the longest x3 1.7 us: shards(): picked = jnp.take(gathered[pair_info[1]], sources[pair_idx], axis=0)]
    slice x2 -> x0, local copies, waits for them, and re-layouts: 1.1 us -> none  [the longest x1 0.55 us: deliver_cols(): partial_value[position].astype(jnp.bfloat16)]
  transfers between devices with their start and end apart: 12 -> 0, of which waited for: 8 -> 0; matrix products, arithmetic and copies ran while one was open for 7% -> 0% of each run, Pallas kernels for 0% -> 0%
where the time goes in v1:
time: 44.1 us; the launch traced here: 43.9 us
  Pallas kernels  42.3 us (96%)
  local copies, waits for them, and re-layouts  1.62 us (4%)
    pallas_call x1, Pallas kernels, shards(): pl.pallas_call(functools.partial(kernel, n_row, n_col), out_shape=jax.Sha...  42.3 us
    unnamed x1, local copies, waits for them, and re-layouts  1.62 us

profile of v1, /device:TPU:0, one launch (start us, length us, event | category | flops | bytes accessed | tf_op | source)
XLA Modules:
  0.0 43.9 jit_solution(17119972947528505838)
XLA Ops:
  0.0 42.3 %shard_map.55 = f32[3,1,1,64,256]{4,3,2,1,0:T(8,128)} custom-call(f32[3,1,1,64,256]{4,3,2,1,0:T(8,128)} %rhs_hbm.1, bf16[3,1,1,256,256]{4,3,2,1,0:T(8,128)(2,1)} %inv_hbm.1, bf16[3,1,10,256,256]{4,3,2,1,0:T(8,128)(2,1)} %fac_hbm.1, s32[3,1,10]{2,1,0:T(1,128)} %tgt_ref.1, s32[3,1,10]{2,1,0:T(1,128)} %src_ref.1), custom_call_target="tpu_custom_call" | custom-call | tf_op jit(solution)/shard_map/pallas_call | solution.py:239
  42.3 1.6 %copy.7 = f32[3,1,1,64,256]{4,3,2,1,0:T(8,128)} copy(f32[3,1,1,64,256]{4,3,2,1,0:T(8,128)} %shard_map.55) | data formatting | bytes 393216

commit v2 on v1

--- a/solution.py
+++ b/solution.py
@@ -25,8 +25,8 @@
     rhs_hbm,
     inv_hbm,
     fac_hbm,
-    tgt_ref,
-    src_ref,
+    tgt_hbm,
+    src_hbm,
     out_ref,
     rhs,
     inv,
@@ -40,8 +40,11 @@
     yfull,
     facc,
     bacc,
+    tgt_ref,
+    src_ref,
     ftab,
     btab,
+    idx_sem,
     rhs_sem,
     inv_sem,
     fac_sem,
@@ -63,6 +66,12 @@
     def col_dev(steps):
         return {"col": lax.rem(me_c + (steps + n_col), n_col)}
 
+    barrier = pltpu.get_barrier_semaphore()
+    for v in row_vals[1:]:
+        pl.semaphore_signal(barrier, inc=1, device_id=row_dev(v), device_id_type=MESH)
+    for v in col_vals[1:]:
+        pl.semaphore_signal(barrier, inc=1, device_id=col_dev(v), device_id_type=MESH)
+
     loads = {}
     for k in range(levels):
         loads["rhs", k] = pltpu.make_async_copy(rhs_hbm.at[k, 0, 0], rhs.at[k], rhs_sem.at[k])
@@ -71,6 +80,10 @@
         loads["fac", p] = pltpu.make_async_copy(fac_hbm.at[p, 0], fac.at[p], fac_sem.at[p])
     loads["rhs", 0].start()
     loads["inv", 0].start()
+    loads["tgt", 0] = pltpu.make_async_copy(tgt_hbm, tgt_ref, idx_sem.at[0])
+    loads["src", 0] = pltpu.make_async_copy(src_hbm, src_ref, idx_sem.at[1])
+    loads["tgt", 0].start()
+    loads["src", 0].start()
     loads["fac", 0].start()
     for k in range(1, levels):
         loads["rhs", k].start()
@@ -83,12 +96,6 @@
         if key not in loaded:
             loads[key].wait()
             loaded.add(key)
-
-    barrier = pltpu.get_barrier_semaphore()
-    for v in row_vals[1:]:
-        pl.semaphore_signal(barrier, inc=1, device_id=row_dev(v), device_id_type=MESH)
-    for v in col_vals[1:]:
-        pl.semaphore_signal(barrier, inc=1, device_id=col_dev(v), device_id_type=MESH)
 
     sends = []
 
@@ -154,6 +161,8 @@
     for lvl in range(levels - 1):
         ycol[lvl][col_w] = jnp.zeros((nrhs, rhs.shape[2]), jnp.bfloat16)
         brow[lvl + 1][row_w] = jnp.zeros((nrhs, rhs.shape[2]), jnp.bfloat16)
+    need("tgt", 0)
+    need("src", 0)
     for p in range(len(pairs)):
         for q in range(slots):
             off_r = tgt_ref[p, 0, q] - me_r
@@ -238,9 +247,8 @@
     bf, f32 = jnp.bfloat16, jnp.float32
     return pl.pallas_call(
         functools.partial(kernel, n_row, n_col),
-        out_shape=jax.ShapeDtypeStruct(rhs.shape, f32),
-        in_specs=[pl.BlockSpec(memory_space=pl.ANY)] * 3
-        + [pl.BlockSpec(memory_space=pltpu.SMEM)] * 2,
+        out_shape=pltpu.VMEM(rhs.shape, f32),
+        in_specs=[pl.BlockSpec(memory_space=pl.ANY)] * 5,
         out_specs=pl.BlockSpec(memory_space=pltpu.VMEM),
         scratch_shapes=[
             pltpu.VMEM((levels, nrhs, size), f32),
@@ -255,8 +263,11 @@
             pltpu.VMEM((levels - 1, nrhs, size), f32),
             pltpu.VMEM((levels, row_w * nrhs, size), f32),
             pltpu.VMEM((levels - 1, col_w * nrhs, size), f32),
+            pltpu.SMEM(tgt.shape, jnp.int32),
+            pltpu.SMEM(src.shape, jnp.int32),
             pltpu.SMEM((pairs, slots, row_w), jnp.int32),
             pltpu.SMEM((pairs, slots, col_w), jnp.int32),
+            pltpu.SemaphoreType.DMA((2,)),
             pltpu.SemaphoreType.DMA((levels,)),
             pltpu.SemaphoreType.DMA((levels,)),
             pltpu.SemaphoreType.DMA((pairs,)),

time: 44.1 us -> 41.7 us (0.946)
  Pallas kernels: 42.3 us -> 40.9 us
  local copies, waits for them, and re-layouts: 1.62 us -> 0.68 us
    pallas_call x1, Pallas kernels: 42.3 us -> 40.9 us  [shards(): pl.pallas_call(functools.partial(kernel, n_row, n_col), out_shape=pltpu.V...]
    unnamed x1, local copies, waits for them, and re-layouts: 1.62 us -> 0.68 us
where the time goes in v2:
time: 41.7 us; the launch traced here: 41.6 us
  Pallas kernels  40.9 us (98%)
  local copies, waits for them, and re-layouts  0.68 us (2%)
    pallas_call x1, Pallas kernels, shards(): pl.pallas_call(functools.partial(kernel, n_row, n_col), out_shape=pltpu.V...  40.9 us

profile of v2, /device:TPU:0, one launch (start us, length us, event | category | flops | bytes accessed | tf_op | source)
XLA Modules:
  0.0 41.6 jit_solution(15030937648496720041)
XLA Ops:
  0.0 40.9 %shard_map.55 = f32[3,1,1,64,256]{4,3,2,1,0:T(8,128)S(1)} custom-call(f32[3,1,1,64,256]{4,3,2,1,0:T(8,128)} %rhs_hbm.1, bf16[3,1,1,256,256]{4,3,2,1,0:T(8,128)(2,1)} %inv_hbm.1, bf16[3,1,10,256,256]{4,3,2,1,0:T(8,128)(2,1)} %fac_hbm.1, s32[3,1,10]{2,1,0:T(1,128)} %tgt_hbm.1, s32[3,1,10]{2,1,0:T(1,128)} %src_hbm.1), custom_call_target="tpu_custom_call" | custom-call | tf_op jit(solution)/shard_map/pallas_call | solution.py:248
  40.9 0.7 %copy.7 = f32[3,1,1,64,256]{4,3,2,1,0:T(8,128)} copy(f32[3,1,1,64,256]{4,3,2,1,0:T(8,128)S(1)} %shard_map.55) | data formatting | bytes 393216

commit v3 on v2

--- a/solution.py
+++ b/solution.py
@@ -8,6 +8,7 @@
 from jax.sharding import PartitionSpec as P
 
 WINDOW = 2
+STREAMS = 2
 MESH = pl.DeviceIdType.MESH
 
 
@@ -53,7 +54,8 @@
 ):
     levels = rhs.shape[0]
     slots = fac.shape[1]
-    nrhs = rhs.shape[1]
+    streams = len(ycol)
+    rows = rhs.shape[1] // streams
     pairs = pair_table(levels)
     row_vals = offset_choices(WINDOW, n_row)
     col_vals = offset_choices(WINDOW, n_col)
@@ -99,12 +101,12 @@
 
     sends = []
 
-    def send(phase, slot, src, dst, device):
+    def send(phase, h, slot, src, dst, device):
         copy = pltpu.make_async_remote_copy(
             src_ref=src,
             dst_ref=dst,
-            send_sem=send_sem.at[phase, slot],
-            recv_sem=recv_sem.at[phase, slot],
+            send_sem=send_sem.at[phase, h, slot],
+            recv_sem=recv_sem.at[phase, h, slot],
             device_id=device,
             device_id_type=MESH,
         )
@@ -125,17 +127,17 @@
         need("fac", p)
         total = None
         for q in range(slots):
-            stacked = jnp.concatenate([panels[table[p, q, j]] for j in range(width)], axis=0)
-            term = dot(stacked, fac[p, q])
+            picks = [ref[table[p, q, j]] for ref in panels for j in range(width)]
+            term = dot(jnp.concatenate(picks, axis=0), fac[p, q])
             total = term if total is None else total + term
         return total
 
-    def spread(phase, vals, device, total, part, recv):
+    def spread(phase, h, vals, device, total, part, recv):
         copies = []
         for k in order(vals):
-            part[k] = total[k * nrhs : (k + 1) * nrhs].astype(jnp.bfloat16)
-            copies.append(send(phase, k, part.at[k], recv.at[k], device(vals[k])))
-        return copies, total[:nrhs].astype(jnp.bfloat16).astype(jnp.float32)
+            part[k] = total[k * rows : (k + 1) * rows].astype(jnp.bfloat16)
+            copies.append(send(phase, h, k, part.at[k], recv.at[k], device(vals[k])))
+        return copies, total[:rows].astype(jnp.bfloat16).astype(jnp.float32)
 
     def collect(copies, recv, own, width):
         for copy in copies:
@@ -144,23 +146,31 @@
             own = own + recv[k].astype(jnp.float32)
         return own
 
-    def share(phase, vals, device, panels):
+    def share(phase, h, vals, device, panels):
         return [
-            send(phase, k, panels.at[0], panels.at[k], device(-vals[k])) for k in order(vals)
+            send(phase, h, k, panels.at[0], panels.at[k], device(-vals[k])) for k in order(vals)
         ]
+
+    everyone = range(streams)
+
+    def part_of(h):
+        return pl.ds(h * rows, rows)
 
     need("rhs", 0)
     need("inv", 0)
     y = dot_t(rhs[0].astype(jnp.bfloat16), inv[0])
     yfull[0] = y
-    ycol[0][0] = y.astype(jnp.bfloat16)
+    for h in everyone:
+        ycol[h][0][0] = y[h * rows : (h + 1) * rows].astype(jnp.bfloat16)
     pl.semaphore_wait(barrier, row_w + col_w - 2)
     phase = 0
-    copies = share(phase, col_vals, col_dev, ycol[0])
-
-    for lvl in range(levels - 1):
-        ycol[lvl][col_w] = jnp.zeros((nrhs, rhs.shape[2]), jnp.bfloat16)
-        brow[lvl + 1][row_w] = jnp.zeros((nrhs, rhs.shape[2]), jnp.bfloat16)
+    copies = [share(phase, h, col_vals, col_dev, ycol[h][0]) for h in everyone]
+
+    zero = jnp.zeros((rows, rhs.shape[2]), jnp.bfloat16)
+    for h in everyone:
+        for lvl in range(levels - 1):
+            ycol[h][lvl][col_w] = zero
+            brow[h][lvl + 1][row_w] = zero
     need("tgt", 0)
     need("src", 0)
     for p in range(len(pairs)):
@@ -181,58 +191,64 @@
                 btab[p, q, k] = jnp.where(pos_c == k, pos_r, row_w)
 
     for k in range(1, levels):
-        total = None
-        for p, (d, s) in enumerate(pairs):
-            if d == k and s == k - 1:
-                for copy in copies:
-                    copy.wait_recv()
-                total = product(p, ycol[s], ftab, row_w, dot_t)
-        if k > 1:
-            total = total + facc[k]
-        phase += 1
-        copies, own = spread(phase, row_vals, row_dev, total, fpart.at[k], frecv.at[k])
+        near = pairs.index((k, k - 1))
+        own = [None] * streams
+        for h in everyone:
+            for copy in copies[h]:
+                copy.wait_recv()
+            total = product(near, [ycol[h][k - 1]], ftab, row_w, dot_t)
+            if k > 1:
+                total = total + facc[k, pl.ds(h * row_w * rows, row_w * rows)]
+            copies[h], own[h] = spread(
+                phase + 1, h, row_vals, row_dev, total, fpart.at[h, k], frecv.at[h, k]
+            )
         for p, (d, s) in enumerate(pairs):
             if s == k - 1 and d > k:
-                later = product(p, ycol[s], ftab, row_w, dot_t)
+                later = product(p, [ycol[h][s] for h in everyone], ftab, row_w, dot_t)
                 facc[d] = later if s == 0 else facc[d] + later
         need("rhs", k)
         need("inv", k)
-        fsum = collect(copies, frecv.at[k], own, row_w)
-        y = dot_t((rhs[k] - fsum).astype(jnp.bfloat16), inv[k])
-        if k < levels - 1:
-            yfull[k] = y
-            ycol[k][0] = y.astype(jnp.bfloat16)
-            phase += 1
-            copies = share(phase, col_vals, col_dev, ycol[k])
+        answers = [None] * streams
+        for h in everyone:
+            fsum = collect(copies[h], frecv.at[h, k], own[h], row_w)
+            y = dot_t((rhs[k, part_of(h)] - fsum).astype(jnp.bfloat16), inv[k])
+            ybf = y.astype(jnp.bfloat16)
+            if k < levels - 1:
+                ycol[h][k][0] = ybf
+                copies[h] = share(phase + 2, h, col_vals, col_dev, ycol[h][k])
+                yfull[k, part_of(h)] = y
+            else:
+                answers[h] = dot_n(ybf, inv[k])
+                brow[h][k][0] = answers[h].astype(jnp.bfloat16)
+                copies[h] = share(phase + 2, h, row_vals, row_dev, brow[h][k])
+                out_ref[k, 0, 0, part_of(h)] = answers[h]
+        phase += 2
 
     top = levels - 1
-    answer = dot_n(y.astype(jnp.bfloat16), inv[top])
-    brow[top][0] = answer.astype(jnp.bfloat16)
-    phase += 1
-    copies = share(phase, row_vals, row_dev, brow[top])
-    out_ref[top, 0, 0] = answer
     for k in reversed(range(top)):
-        total = None
-        for p, (d, s) in enumerate(pairs):
-            if s == k and d == k + 1:
-                for copy in copies:
-                    copy.wait_recv()
-                total = product(p, brow[d], btab, col_w, dot_n)
-        if k + 1 < top:
-            total = total + bacc[k]
-        phase += 1
-        copies, own = spread(phase, col_vals, col_dev, total, bpart.at[k], brecv.at[k])
+        near = pairs.index((k + 1, k))
+        own = [None] * streams
+        for h in everyone:
+            for copy in copies[h]:
+                copy.wait_recv()
+            total = product(near, [brow[h][k + 1]], btab, col_w, dot_n)
+            if k + 1 < top:
+                total = total + bacc[k, pl.ds(h * col_w * rows, col_w * rows)]
+            copies[h], own[h] = spread(
+                phase + 1, h, col_vals, col_dev, total, bpart.at[h, k], brecv.at[h, k]
+            )
         for p, (d, s) in enumerate(pairs):
             if d == k + 1 and s < k:
-                later = product(p, brow[d], btab, col_w, dot_n)
+                later = product(p, [brow[h][d] for h in everyone], btab, col_w, dot_n)
                 bacc[s] = later if d == top else bacc[s] + later
-        bsum = collect(copies, brecv.at[k], own, col_w)
-        answer = dot_n((yfull[k] - bsum).astype(jnp.bfloat16), inv[k])
-        if k > 0:
-            brow[k][0] = answer.astype(jnp.bfloat16)
-            phase += 1
-            copies = share(phase, row_vals, row_dev, brow[k])
-        out_ref[k, 0, 0] = answer
+        for h in everyone:
+            bsum = collect(copies[h], brecv.at[h, k], own[h], col_w)
+            answer = dot_n((yfull[k, part_of(h)] - bsum).astype(jnp.bfloat16), inv[k])
+            if k > 0:
+                brow[h][k][0] = answer.astype(jnp.bfloat16)
+                copies[h] = share(phase + 2, h, row_vals, row_dev, brow[h][k])
+            out_ref[k, 0, 0, part_of(h)] = answer
+        phase += 2
     for copy in sends:
         copy.wait_send()
 
@@ -244,6 +260,7 @@
     col_w = len(offset_choices(WINDOW, n_col))
     width = max(row_w, col_w)
     phases = 4 * (levels - 1)
+    rows = nrhs // STREAMS
     bf, f32 = jnp.bfloat16, jnp.float32
     return pl.pallas_call(
         functools.partial(kernel, n_row, n_col),
@@ -254,12 +271,12 @@
             pltpu.VMEM((levels, nrhs, size), f32),
             pltpu.VMEM((levels, size, size), bf),
             pltpu.VMEM((pairs, slots, size, size), bf),
-            [pltpu.VMEM((col_w + 1, nrhs, size), bf)] * (levels - 1),
-            [pltpu.VMEM((row_w + 1, nrhs, size), bf)] * levels,
-            pltpu.VMEM((levels, row_w, nrhs, size), bf),
-            pltpu.VMEM((levels, row_w, nrhs, size), bf),
-            pltpu.VMEM((levels - 1, col_w, nrhs, size), bf),
-            pltpu.VMEM((levels - 1, col_w, nrhs, size), bf),
+            [[pltpu.VMEM((col_w + 1, rows, size), bf)] * (levels - 1)] * STREAMS,
+            [[pltpu.VMEM((row_w + 1, rows, size), bf)] * levels] * STREAMS,
+            pltpu.VMEM((STREAMS, levels, row_w, rows, size), bf),
+            pltpu.VMEM((STREAMS, levels, row_w, rows, size), bf),
+            pltpu.VMEM((STREAMS, levels - 1, col_w, rows, size), bf),
+            pltpu.VMEM((STREAMS, levels - 1, col_w, rows, size), bf),
             pltpu.VMEM((levels - 1, nrhs, size), f32),
             pltpu.VMEM((levels, row_w * nrhs, size), f32),
             pltpu.VMEM((levels - 1, col_w * nrhs, size), f32),
@@ -271,8 +288,8 @@
             pltpu.SemaphoreType.DMA((levels,)),
             pltpu.SemaphoreType.DMA((levels,)),
             pltpu.SemaphoreType.DMA((pairs,)),
-            pltpu.SemaphoreType.DMA((phases, width)),
-            pltpu.SemaphoreType.DMA((phases, width)),
+            pltpu.SemaphoreType.DMA((phases, STREAMS, width)),
+            pltpu.SemaphoreType.DMA((phases, STREAMS, width)),
         ],
         compiler_params=pltpu.CompilerParams(collective_id=0, has_side_effects=True),
     )(rhs, inv, fac, tgt, src)

time: 41.7 us -> 39.6 us (0.950)
  Pallas kernels: 40.9 us -> 38.8 us
    pallas_call x1, Pallas kernels: 40.9 us -> 38.8 us  [shards(): pl.pallas_call(functools.partial(kernel, n_row, n_col), out_shape=pltpu.V...]
where the time goes in v3:
time: 39.6 us; the launch traced here: 39.4 us
  Pallas kernels  38.8 us (98%)
  local copies, waits for them, and re-layouts  0.68 us (2%)
    pallas_call x1, Pallas kernels, shards(): pl.pallas_call(functools.partial(kernel, n_row, n_col), out_shape=pltpu.V...  38.8 us

profile of v3, /device:TPU:0, one launch (start us, length us, event | category | flops | bytes accessed | tf_op | source)
XLA Modules:
  0.0 39.4 jit_solution(12715221664923535915)
XLA Ops:
  0.0 38.8 %shard_map.55 = f32[3,1,1,64,256]{4,3,2,1,0:T(8,128)S(1)} custom-call(f32[3,1,1,64,256]{4,3,2,1,0:T(8,128)} %rhs_hbm.1, bf16[3,1,1,256,256]{4,3,2,1,0:T(8,128)(2,1)} %inv_hbm.1, bf16[3,1,10,256,256]{4,3,2,1,0:T(8,128)(2,1)} %fac_hbm.1, s32[3,1,10]{2,1,0:T(1,128)} %tgt_hbm.1, s32[3,1,10]{2,1,0:T(1,128)} %src_hbm.1), custom_call_target="tpu_custom_call" | custom-call | tf_op jit(solution)/shard_map/pallas_call | solution.py:265
  38.8 0.7 %copy.7 = f32[3,1,1,64,256]{4,3,2,1,0:T(8,128)} copy(f32[3,1,1,64,256]{4,3,2,1,0:T(8,128)S(1)} %shard_map.55) | data formatting | bytes 393216

commit v4 on v3

--- a/solution.py
+++ b/solution.py
@@ -99,20 +99,19 @@
             loads[key].wait()
             loaded.add(key)
 
-    sends = []
-
-    def send(phase, h, slot, src, dst, device):
-        copy = pltpu.make_async_remote_copy(
+    def send(phase, h, src, dst, device):
+        pltpu.make_async_remote_copy(
             src_ref=src,
             dst_ref=dst,
-            send_sem=send_sem.at[phase, h, slot],
-            recv_sem=recv_sem.at[phase, h, slot],
+            send_sem=send_sem.at[0],
+            recv_sem=recv_sem.at[phase, h],
             device_id=device,
             device_id_type=MESH,
-        )
-        copy.start()
-        sends.append(copy)
-        return copy
+        ).start()
+
+    def arrive(phase, h, landed, width):
+        slabs = landed.at[pl.ds(1, width - 1)]
+        pltpu.make_async_copy(slabs, slabs, recv_sem.at[phase, h]).wait()
 
     def dot_t(a, b):
         return lax.dot_general(a, b, (((1,), (1,)), ((), ())), preferred_element_type=jnp.float32)
@@ -133,23 +132,20 @@
         return total
 
     def spread(phase, h, vals, device, total, part, recv):
-        copies = []
         for k in order(vals):
             part[k] = total[k * rows : (k + 1) * rows].astype(jnp.bfloat16)
-            copies.append(send(phase, h, k, part.at[k], recv.at[k], device(vals[k])))
-        return copies, total[:rows].astype(jnp.bfloat16).astype(jnp.float32)
-
-    def collect(copies, recv, own, width):
-        for copy in copies:
-            copy.wait_recv()
+            send(phase, h, part.at[k], recv.at[k], device(vals[k]))
+        return total[:rows].astype(jnp.bfloat16).astype(jnp.float32)
+
+    def collect(phase, h, recv, own, width):
+        arrive(phase, h, recv, width)
         for k in range(1, width):
             own = own + recv[k].astype(jnp.float32)
         return own
 
     def share(phase, h, vals, device, panels):
-        return [
-            send(phase, h, k, panels.at[0], panels.at[k], device(-vals[k])) for k in order(vals)
-        ]
+        for k in order(vals):
+            send(phase, h, panels.at[0], panels.at[k], device(-vals[k]))
 
     everyone = range(streams)
 
@@ -164,7 +160,8 @@
         ycol[h][0][0] = y[h * rows : (h + 1) * rows].astype(jnp.bfloat16)
     pl.semaphore_wait(barrier, row_w + col_w - 2)
     phase = 0
-    copies = [share(phase, h, col_vals, col_dev, ycol[h][0]) for h in everyone]
+    for h in everyone:
+        share(phase, h, col_vals, col_dev, ycol[h][0])
 
     zero = jnp.zeros((rows, rhs.shape[2]), jnp.bfloat16)
     for h in everyone:
@@ -194,12 +191,11 @@
         near = pairs.index((k, k - 1))
         own = [None] * streams
         for h in everyone:
-            for copy in copies[h]:
-                copy.wait_recv()
+            arrive(phase, h, ycol[h][k - 1], col_w)
             total = product(near, [ycol[h][k - 1]], ftab, row_w, dot_t)
             if k > 1:
                 total = total + facc[k, pl.ds(h * row_w * rows, row_w * rows)]
-            copies[h], own[h] = spread(
+            own[h] = spread(
                 phase + 1, h, row_vals, row_dev, total, fpart.at[h, k], frecv.at[h, k]
             )
         for p, (d, s) in enumerate(pairs):
@@ -210,17 +206,17 @@
         need("inv", k)
         answers = [None] * streams
         for h in everyone:
-            fsum = collect(copies[h], frecv.at[h, k], own[h], row_w)
+            fsum = collect(phase + 1, h, frecv.at[h, k], own[h], row_w)
             y = dot_t((rhs[k, part_of(h)] - fsum).astype(jnp.bfloat16), inv[k])
             ybf = y.astype(jnp.bfloat16)
             if k < levels - 1:
                 ycol[h][k][0] = ybf
-                copies[h] = share(phase + 2, h, col_vals, col_dev, ycol[h][k])
+                share(phase + 2, h, col_vals, col_dev, ycol[h][k])
                 yfull[k, part_of(h)] = y
             else:
                 answers[h] = dot_n(ybf, inv[k])
                 brow[h][k][0] = answers[h].astype(jnp.bfloat16)
-                copies[h] = share(phase + 2, h, row_vals, row_dev, brow[h][k])
+                share(phase + 2, h, row_vals, row_dev, brow[h][k])
                 out_ref[k, 0, 0, part_of(h)] = answers[h]
         phase += 2
 
@@ -229,12 +225,11 @@
         near = pairs.index((k + 1, k))
         own = [None] * streams
         for h in everyone:
-            for copy in copies[h]:
-                copy.wait_recv()
+            arrive(phase, h, brow[h][k + 1], row_w)
             total = product(near, [brow[h][k + 1]], btab, col_w, dot_n)
             if k + 1 < top:
                 total = total + bacc[k, pl.ds(h * col_w * rows, col_w * rows)]
-            copies[h], own[h] = spread(
+            own[h] = spread(
                 phase + 1, h, col_vals, col_dev, total, bpart.at[h, k], brecv.at[h, k]
             )
         for p, (d, s) in enumerate(pairs):
@@ -242,15 +237,16 @@
                 later = product(p, [brow[h][d] for h in everyone], btab, col_w, dot_n)
                 bacc[s] = later if d == top else bacc[s] + later
         for h in everyone:
-            bsum = collect(copies[h], brecv.at[h, k], own[h], col_w)
+            bsum = collect(phase + 1, h, brecv.at[h, k], own[h], col_w)
             answer = dot_n((yfull[k, part_of(h)] - bsum).astype(jnp.bfloat16), inv[k])
             if k > 0:
                 brow[h][k][0] = answer.astype(jnp.bfloat16)
-                copies[h] = share(phase + 2, h, row_vals, row_dev, brow[h][k])
+                share(phase + 2, h, row_vals, row_dev, brow[h][k])
             out_ref[k, 0, 0, part_of(h)] = answer
         phase += 2
-    for copy in sends:
-        copy.wait_send()
+    panels_sent = (levels - 1) * 2 * (row_w + col_w - 2)
+    sent = fac.at[0, pl.ds(0, panels_sent * rhs.shape[1] // fac.shape[2])]
+    pltpu.make_async_copy(sent, sent, send_sem.at[0]).wait()
 
 
 def shards(n_row, n_col, rhs, inv, fac, tgt, src):
@@ -258,7 +254,6 @@
     pairs, slots = fac.shape[0], fac.shape[2]
     row_w = len(offset_choices(WINDOW, n_row))
     col_w = len(offset_choices(WINDOW, n_col))
-    width = max(row_w, col_w)
     phases = 4 * (levels - 1)
     rows = nrhs // STREAMS
     bf, f32 = jnp.bfloat16, jnp.float32
@@ -288,8 +283,8 @@
             pltpu.SemaphoreType.DMA((levels,)),
             pltpu.SemaphoreType.DMA((levels,)),
             pltpu.SemaphoreType.DMA((pairs,)),
-            pltpu.SemaphoreType.DMA((phases, STREAMS, width)),
-            pltpu.SemaphoreType.DMA((phases, STREAMS, width)),
+            pltpu.SemaphoreType.DMA((1,)),
+            pltpu.SemaphoreType.DMA((phases, STREAMS)),
         ],
         compiler_params=pltpu.CompilerParams(collective_id=0, has_side_effects=True),
     )(rhs, inv, fac, tgt, src)

time: 39.6 us -> 38.5 us (0.972)
  Pallas kernels: 38.8 us -> 37.7 us
    pallas_call x1, Pallas kernels: 38.8 us -> 37.7 us  [shards(): pl.pallas_call(functools.partial(kernel, n_row, n_col), out_shape=pltpu.V...]
where the time goes in v4:
time: 38.5 us; the launch traced here: 38.4 us
  Pallas kernels  37.7 us (98%)
  local copies, waits for them, and re-layouts  0.68 us (2%)
    pallas_call x1, Pallas kernels, shards(): pl.pallas_call(functools.partial(kernel, n_row, n_col), out_shape=pltpu.V...  37.7 us

profile of v4, /device:TPU:0, one launch (start us, length us, event | category | flops | bytes accessed | tf_op | source)
XLA Modules:
  0.0 38.4 jit_solution(9295675188651812764)
XLA Ops:
  0.0 37.7 %shard_map.55 = f32[3,1,1,64,256]{4,3,2,1,0:T(8,128)S(1)} custom-call(f32[3,1,1,64,256]{4,3,2,1,0:T(8,128)} %rhs_hbm.1, bf16[3,1,1,256,256]{4,3,2,1,0:T(8,128)(2,1)} %inv_hbm.1, bf16[3,1,10,256,256]{4,3,2,1,0:T(8,128)(2,1)} %fac_hbm.1, s32[3,1,10]{2,1,0:T(1,128)} %tgt_hbm.1, s32[3,1,10]{2,1,0:T(1,128)} %src_hbm.1), custom_call_target="tpu_custom_call" | custom-call | tf_op jit(solution)/shard_map/pallas_call | solution.py:260
  37.7 0.7 %copy.7 = f32[3,1,1,64,256]{4,3,2,1,0:T(8,128)} copy(f32[3,1,1,64,256]{4,3,2,1,0:T(8,128)S(1)} %shard_map.55) | data formatting | bytes 393216

commit v5 on v4

--- a/solution.py
+++ b/solution.py
@@ -131,10 +131,41 @@
             total = term if total is None else total + term
         return total
 
+    def turns(vals, me, count, sign):
+        slots_left = list(range(1, len(vals)))
+        far = []
+        for k in slots_left:
+            peer = lax.rem(me + (sign * vals[k] + count), count)
+            far.append(jnp.abs(peer - me))
+        ranks = []
+        for i, k in enumerate(slots_left):
+            rank = jnp.int32(0)
+            for j in range(len(slots_left)):
+                if j < i:
+                    rank = rank + jnp.where(far[j] >= far[i], 1, 0)
+                elif j > i:
+                    rank = rank + jnp.where(far[j] > far[i], 1, 0)
+            ranks.append(rank)
+        picked = []
+        for turn in range(len(slots_left)):
+            k_now, v_now = jnp.int32(0), jnp.int32(0)
+            for i, k in enumerate(slots_left):
+                k_now = jnp.where(ranks[i] == turn, k, k_now)
+                v_now = jnp.where(ranks[i] == turn, vals[k], v_now)
+            picked.append((k_now, v_now))
+        return picked
+
+    row_out = turns(row_vals, me_r, n_row, 1)
+    row_back = turns(row_vals, me_r, n_row, -1)
+
     def spread(phase, h, vals, device, total, part, recv):
         for k in order(vals):
             part[k] = total[k * rows : (k + 1) * rows].astype(jnp.bfloat16)
-            send(phase, h, part.at[k], recv.at[k], device(vals[k]))
+            if device is col_dev:
+                send(phase, h, part.at[k], recv.at[k], device(vals[k]))
+        if device is row_dev:
+            for k, v in row_out:
+                send(phase, h, part.at[k], recv.at[k], device(v))
         return total[:rows].astype(jnp.bfloat16).astype(jnp.float32)
 
     def collect(phase, h, recv, own, width):
@@ -144,8 +175,12 @@
         return own
 
     def share(phase, h, vals, device, panels):
-        for k in order(vals):
-            send(phase, h, panels.at[0], panels.at[k], device(-vals[k]))
+        if device is row_dev:
+            for k, v in row_back:
+                send(phase, h, panels.at[0], panels.at[k], device(-v))
+        else:
+            for k in order(vals):
+                send(phase, h, panels.at[0], panels.at[k], device(-vals[k]))
 
     everyone = range(streams)
 

time: 38.5 us -> 37.5 us (0.974)
  Pallas kernels: 37.7 us -> 36.4 us
    pallas_call x1, Pallas kernels: 37.7 us -> 36.4 us  [shards(): pl.pallas_call(functools.partial(kernel, n_row, n_col), out_shape=pltpu.V...]
where the time goes in v5:
time: 37.5 us; the launch traced here: 37 us
  Pallas kernels  36.4 us (97%)
  local copies, waits for them, and re-layouts  0.68 us (2%)
    pallas_call x1, Pallas kernels, shards(): pl.pallas_call(functools.partial(kernel, n_row, n_col), out_shape=pltpu.V...  36.4 us

profile of v5, /device:TPU:0, one launch (start us, length us, event | category | flops | bytes accessed | tf_op | source)
XLA Modules:
  0.0 37.0 jit_solution(4025685662691330241)
XLA Ops:
  0.0 36.4 %shard_map.55 = f32[3,1,1,64,256]{4,3,2,1,0:T(8,128)S(1)} custom-call(f32[3,1,1,64,256]{4,3,2,1,0:T(8,128)} %rhs_hbm.1, bf16[3,1,1,256,256]{4,3,2,1,0:T(8,128)(2,1)} %inv_hbm.1, bf16[3,1,10,256,256]{4,3,2,1,0:T(8,128)(2,1)} %fac_hbm.1, s32[3,1,10]{2,1,0:T(1,128)} %tgt_hbm.1, s32[3,1,10]{2,1,0:T(1,128)} %src_hbm.1), custom_call_target="tpu_custom_call" | custom-call | tf_op jit(solution)/shard_map/pallas_call | solution.py:295
  36.4 0.7 %copy.7 = f32[3,1,1,64,256]{4,3,2,1,0:T(8,128)} copy(f32[3,1,1,64,256]{4,3,2,1,0:T(8,128)S(1)} %shard_map.55) | data formatting | bytes 393216

commit v6 on v5

--- a/solution.py
+++ b/solution.py
@@ -68,12 +68,6 @@
     def col_dev(steps):
         return {"col": lax.rem(me_c + (steps + n_col), n_col)}
 
-    barrier = pltpu.get_barrier_semaphore()
-    for v in row_vals[1:]:
-        pl.semaphore_signal(barrier, inc=1, device_id=row_dev(v), device_id_type=MESH)
-    for v in col_vals[1:]:
-        pl.semaphore_signal(barrier, inc=1, device_id=col_dev(v), device_id_type=MESH)
-
     loads = {}
     for k in range(levels):
         loads["rhs", k] = pltpu.make_async_copy(rhs_hbm.at[k, 0, 0], rhs.at[k], rhs_sem.at[k])
@@ -82,6 +76,12 @@
         loads["fac", p] = pltpu.make_async_copy(fac_hbm.at[p, 0], fac.at[p], fac_sem.at[p])
     loads["rhs", 0].start()
     loads["inv", 0].start()
+    barrier = pltpu.get_barrier_semaphore()
+    for v in row_vals[1:]:
+        pl.semaphore_signal(barrier, inc=1, device_id=row_dev(v), device_id_type=MESH)
+    for v in col_vals[1:]:
+        pl.semaphore_signal(barrier, inc=1, device_id=col_dev(v), device_id_type=MESH)
+
     loads["tgt", 0] = pltpu.make_async_copy(tgt_hbm, tgt_ref, idx_sem.at[0])
     loads["src", 0] = pltpu.make_async_copy(src_hbm, src_ref, idx_sem.at[1])
     loads["tgt", 0].start()

time: 37.5 us -> 37.5 us (level)
  no operation moved by 1% of the time
where the time goes in v6:
time: 37.5 us; the launch traced here: 37 us
  Pallas kernels  36.4 us (97%)
  local copies, waits for them, and re-layouts  0.68 us (2%)
    pallas_call x1, Pallas kernels, shards(): pl.pallas_call(functools.partial(kernel, n_row, n_col), out_shape=pltpu.V...  36.4 us

profile of v6, /device:TPU:0, one launch (start us, length us, event | category | flops | bytes accessed | tf_op | source)
XLA Modules:
  0.0 37.0 jit_solution(12030217093459214542)
XLA Ops:
  0.0 36.4 %shard_map.55 = f32[3,1,1,64,256]{4,3,2,1,0:T(8,128)S(1)} custom-call(f32[3,1,1,64,256]{4,3,2,1,0:T(8,128)} %rhs_hbm.1, bf16[3,1,1,256,256]{4,3,2,1,0:T(8,128)(2,1)} %inv_hbm.1, bf16[3,1,10,256,256]{4,3,2,1,0:T(8,128)(2,1)} %fac_hbm.1, s32[3,1,10]{2,1,0:T(1,128)} %tgt_hbm.1, s32[3,1,10]{2,1,0:T(1,128)} %src_hbm.1), custom_call_target="tpu_custom_call" | custom-call | tf_op jit(solution)/shard_map/pallas_call | solution.py:295
  36.4 0.7 %copy.7 = f32[3,1,1,64,256]{4,3,2,1,0:T(8,128)} copy(f32[3,1,1,64,256]{4,3,2,1,0:T(8,128)S(1)} %shard_map.55) | data formatting | bytes 393216
